TPU v7x, 128 devices: a whole 4x4x4 slice. The times are simulated.
128 devices in a mesh: wide: 16 (over z, x), narrow: 8 (over y, core).
Axes of the slice: x: 4, y: 4, z: 4, core: 2. Of those that a mesh axis runs over, the one named last changes fastest.
Arguments:
- state: float32 [12, 256, 128, 128], P(None, 'wide', 'narrow'), may hold values from -6 to 6
- wind_x: bfloat16 [256, 128, 128], P('wide', 'narrow'), may hold values from -8 to 8
- wind_y: bfloat16 [256, 128, 128], P('wide', 'narrow'), may hold values from -8 to 8
- level_mix: bfloat16 [128, 128], replicated, may hold values from -0.5 to 0.5
- field_mix: float32 [12, 12], replicated, may hold values from -1.75 to 1.75
- block_cost: int32 [32, 8], P('wide', 'narrow'), may hold values from 6 to 24
Outputs:
- new_state: float32 [12, 256, 128, 128], P(None, 'wide', 'narrow')
- tendency: float32 [12, 256, 128, 128], P(None, 'wide', 'narrow')
All inputs are finite; a program needn't handle non-finite values.
Results may differ from a plain program's by a relative error of at most 0.0012.
Values sent between devices are 32-bit elements; how exact they have to be, the bound alone decides.
No kernel may reach another device: no remote copies, remote signals or barrier semaphores. Data moves between devices by JAX's collectives and lax.ppermute only.
A program may use at most 64 MiB of HBM per device.

v0:
```python
import functools
import math

import jax
import jax.numpy as jnp
import numpy as np
from jax import lax
from jax.experimental import pallas as pl
from jax.experimental.pallas import tpu as pltpu
from jax.sharding import PartitionSpec as P


NV = 12
NF = NV + 1
LEV = 128
N = 16
NSUB = 4
STEP = 0.05
F32 = jnp.float32
BF16 = jnp.bfloat16
EXTRA = 8


def derivative_numbers():
    nodes = np.array([-1.0, -1.0 / math.sqrt(5.0), 1.0 / math.sqrt(5.0), 1.0])
    spacing = nodes[:, None] - nodes[None, :] + np.eye(4)
    weights = 1.0 / np.prod(spacing, axis=1)
    off = weights[None, :] / weights[:, None] / spacing * (1.0 - np.eye(4))
    return off - np.diag(off.sum(1))


DER = derivative_numbers()
COPIES = np.array([2.0, 1.0, 1.0, 2.0])
DERC = DER / COPIES[:, None]


def vmem():
    return pl.BlockSpec(memory_space=pltpu.VMEM)


def call(body, ins, outs, micros, aliases=None, scratch=(), smem=0, hbm=0):
    specs = [pl.BlockSpec(memory_space=pltpu.SMEM)] * smem
    specs += [pl.BlockSpec(memory_space=pltpu.HBM)] * hbm
    specs += [vmem()] * (len(ins) - smem - hbm)
    return pl.pallas_call(
      body,
      out_shape=tuple(jax.ShapeDtypeStruct(s, F32) for s in outs),
      in_specs=specs,
      out_specs=tuple(vmem() for _ in outs),
      scratch_shapes=list(scratch),
      input_output_aliases=aliases or {},
      compiler_params=pltpu.CompilerParams(vmem_limit_bytes=6 << 20),
      cost_estimate=pl.CostEstimate(
          flops=int(micros * 4e6), bytes_accessed=int(micros * 2e6), transcendentals=0
      ),
    )(*ins)


def field_operator(field_mix):
    row = lax.broadcasted_iota(jnp.int32, (96, NV), 0) // 8
    pick = (row == lax.broadcasted_iota(jnp.int32, (96, NV), 1)).astype(F32)
    wide = lax.dot_general(
        pick, field_mix, (((1,), (0,)), ((), ())),
        precision=lax.Precision.HIGHEST, preferred_element_type=F32,
    )
    wide = lax.dot_general(
        wide, pick, (((1,), (1,)), ((), ())),
        precision=lax.Precision.HIGHEST, preferred_element_type=F32,
    )
    left = lax.broadcasted_iota(jnp.int32, (96, 96), 0) % 8
    right = lax.broadcasted_iota(jnp.int32, (96, 96), 1) % 8
    wide = jnp.where(left == right, wide, 0.0)
    high = wide.astype(BF16)
    low = (wide - high.astype(F32)).astype(BF16)
    return high, low


def physics_body(
    count_ref, state_ref, level_ref, mix_ref, moved_ref,
    raw_ref, sum_ref, s_ref, field_w, level_w,
):
    high, low = field_operator(mix_ref[...])
    field_w[:, :96] = high
    field_w[:, 96:192] = low
    field_w[:, 192:] = high[:, : 8 * EXTRA]
    level_w[...] = jnp.zeros_like(level_w)
    level_w[:LEV, :LEV] = level_ref[...]
    level_w[LEV:, LEV:] = level_ref[...]
    raw_ref[...] = state_ref[...]

    def part(row, half):
        return (slice(None), slice(16 * row + 8 * half, 16 * row + 8 * half + 8), slice(None))

    def turn(rows):
        now = [[raw_ref[part(r, h)].reshape(96, LEV) for h in range(2)] for r in rows]
        packed = [jnp.concatenate([x.astype(BF16) for x in pair], axis=1) for pair in now]
        mixed = jnp.dot(
            jnp.concatenate(packed, axis=0), level_w[...], preferred_element_type=F32
        )
        for i, r in enumerate(rows):
            y = mixed[96 * i : 96 * i + 96]
            y_high = y.astype(BF16)
            y_low = (y[: 8 * EXTRA] - y_high[: 8 * EXTRA].astype(F32)).astype(BF16)
            coupled = jnp.dot(
                field_w[...],
                jnp.concatenate([y_high, y_high, y_low], axis=0),
                preferred_element_type=F32,
            )
            for h in range(2):
                value = jnp.tanh(coupled[:, LEV * h : LEV * h + LEV])
                raw_ref[part(r, h)] = (0.5 * (now[i][h] + value)).reshape(NV, 8, LEV)

    first = count_ref[0, 0]
    second = count_ref[1, 0]
    both = jnp.minimum(first, second)

    def joint(i, carry):
        turn(range(16))
        return carry

    lax.fori_loop(0, both, joint, 0)
    for block, count in ((0, first), (1, second)):

        def single(i, carry, block=block):
            turn(range(8 * block, 8 * block + 8))
            return carry

        lax.fori_loop(both, count, single, 0)

    def finish(v, carry):
        raw = raw_ref[v] - state_ref[v]
        raw_ref[v] = raw
        s_ref[v] = moved_ref[v] + STEP * raw
        sum_ref[pl.ds(v, 1), :] = jnp.sum(raw, axis=0, keepdims=True)
        return carry

    lax.fori_loop(0, NV, finish, 0, unroll=2)
    s_ref[NV] = jnp.full((256, LEV), STEP, F32)


def column_table(shift):
    b = lax.broadcasted_iota(jnp.int32, (8, LEV), 0) % 4
    out = jnp.full((8, LEV), float(DERC[3, 3 ^ shift]), F32)
    for k in range(3):
        out = jnp.where(b == k, float(DERC[k, k ^ shift]), out)
    return out


def tables():
    return [column_table(s) for s in range(4)]


def permuted(x, index):
    return jnp.take_along_axis(x, index, axis=0)


def indices():
    q = lax.broadcasted_iota(jnp.int32, (8, LEV), 0)
    return [q ^ s for s in range(4)]


def along_sublanes(x, coef, index):
    out = coef[0] * x
    for s in range(1, 4):
        out = out + coef[s] * permuted(x, index[s])
    return out


def column_edges(s_ref, v, edge_ref, side, half, coef, index):
    q0 = 0 if side == 0 else 12
    edge = 0 if side == 0 else 3
    rows = []
    for j in range(4):
        rows.append(s_ref[v, pl.ds(128 * half + q0 + j, 8, stride=16), :])
    out = along_sublanes(edge_ref[side, 4, pl.ds(8 * half, 8), :] * rows[edge], coef, index)
    for j in range(4):
        out = out + edge_ref[side, j, pl.ds(8 * half, 8), :] * rows[j]
    return out


def write_edges(fields, s_ref, edge_ref, left_ref, right_ref):
    coef, index = tables(), indices()

    def one(v, carry):
        for side, ref in ((0, left_ref), (1, right_ref)):
            for half in range(2):
                ref[v, pl.ds(8 * half, 8), :] = column_edges(
                    s_ref, v, edge_ref, side, half, coef, index
                )
        return carry

    lax.fori_loop(0, fields, one, 0)


def first_body(
    state_hbm, wx_hbm, wy_hbm, s_ref, wxs_ref, wys_ref, edge_ref, left_ref, right_ref,
    wx_ref, wy_ref, sems,
):
    winds = [
        pltpu.make_async_copy(wx_hbm, wx_ref, sems.at[NV]),
        pltpu.make_async_copy(wy_hbm, wy_ref, sems.at[NV + 1]),
    ]
    fields = [
        pltpu.make_async_copy(state_hbm.at[v], s_ref.at[v], sems.at[v]) for v in range(NV)
    ]
    for copy in winds + fields:
        copy.start()
    for copy in winds:
        copy.wait()
    q = lax.broadcasted_iota(jnp.int32, (16, LEV), 0) % 4
    inner = (q == 1) | (q == 2)
    per_q = jnp.where(inner, -STEP, -0.5 * STEP)
    for p in range(N):
        rows = pl.ds(16 * p, 16)
        wxs_ref[rows, :] = per_q * wx_ref[rows, :].astype(F32)
        wys_ref[rows, :] = float(-STEP / COPIES[p % 4]) * wy_ref[rows, :].astype(F32)
    for side in range(2):
        q0, edge = (0, 0) if side == 0 else (12, 3)
        for half in range(2):
            at = pl.ds(8 * half, 8)
            for j in range(4):
                wind = wys_ref[pl.ds(128 * half + q0 + j, 8, stride=16), :]
                edge_ref[side, j, at, :] = float(DERC[edge, j]) * wind
            edge_ref[side, 4, at, :] = wxs_ref[pl.ds(128 * half + q0 + edge, 8, stride=16), :]
    for copy in fields:
        copy.wait()
    write_edges(NV, s_ref, edge_ref, left_ref, right_ref)


def along_rows(f):
    c = DERC
    plus, minus = f[0] + f[3], f[0] - f[3]
    inner_plus, inner_minus = f[1] + f[2], f[1] - f[2]
    even = plus - inner_plus
    a = float(0.5 * (c[0, 0] - c[0, 3])) * minus + float(0.5 * (c[0, 1] - c[0, 2])) * inner_minus
    b = float(0.5 * (c[0, 0] + c[0, 3])) * even
    d = float(0.5 * (c[1, 0] - c[1, 3])) * minus + float(0.5 * (c[1, 1] - c[1, 2])) * inner_minus
    e = float(0.5 * (c[1, 0] + c[1, 3])) * even
    return [a + b, d + e, d - e, a - b]


def full_body(fields, s_ref, wxs_ref, wys_ref, *refs):
    if len(refs) == 3:
        refs[2][...] = refs[0][...]
    g_ref = refs[len(refs) // 2]
    coef, index = tables(), indices()
    q = lax.broadcasted_iota(jnp.int32, (8, LEV), 0)
    middle = (q == 3) | (q == 4)
    low, high = q == 0, q == 7
    swap = jnp.where(low, 7, jnp.where(high, 0, jnp.where(middle, 7 - q, q)))

    def one(v, carry):
        for e in range(4):
            halves = []
            for half in range(2):
                at = [pl.ds(64 * e + 16 * a + 8 * half, 8) for a in range(4)]
                s = [s_ref[v, at[a], :] for a in range(4)]
                x = along_rows([wxs_ref[at[a], :] * s[a] for a in range(4)])
                halves.append(
                    [
                        x[a] + along_sublanes(wys_ref[at[a], :] * s[a], coef, index)
                        for a in range(4)
                    ]
                )
            for a in range(4):
                left, right = halves[0][a], halves[1][a]
                p_left, p_right = permuted(left, swap), permuted(right, swap)
                left = left + jnp.where(high, p_right, jnp.where(middle, p_left, 0.0))
                right = right + jnp.where(low, p_left, jnp.where(middle, p_right, 0.0))
                g_ref[v, pl.ds(64 * e + 16 * a, 8), :] = left
                g_ref[v, pl.ds(64 * e + 16 * a + 8, 8), :] = right
        return carry

    lax.fori_loop(0, fields, one, 0)


def with_columns(g_ref, from_left, from_right, v, p, low, high):
    left = g_ref[v, pl.ds(16 * p, 8), :]
    right = g_ref[v, pl.ds(16 * p + 8, 8), :]
    left = left + jnp.where(low, from_left[v, pl.ds(p, 1), :], 0.0)
    right = right + jnp.where(high, from_right[v, pl.ds(p, 1), :], 0.0)
    return left, right


def ends():
    q = lax.broadcasted_iota(jnp.int32, (8, LEV), 0)
    return q == 0, q == 7


def rows_body(fields, g_ref, from_left, from_right, top_ref, bottom_ref):
    low, high = ends()

    def one(v, carry):
        for p, ref in ((0, top_ref), (N - 1, bottom_ref)):
            left, right = with_columns(g_ref, from_left, from_right, v, p, low, high)
            ref[v, 0:8, :] = left
            ref[v, 8:16, :] = right
        return carry

    lax.fori_loop(0, fields, one, 0)


def advance(s_ref, g_ref, from_left, from_right, v, low, high, source, out_ref, inner=False):
    g = [with_columns(g_ref, from_left, from_right, v, p, low, high) for p in range(N)]
    for p in range(N):
        mate = p + 1 if p % 4 == 3 else p - 1 if p % 4 == 0 else -1
        for half in range(2):
            at = pl.ds(16 * p + 8 * half, 8)
            value = g[p][half]
            if 0 <= mate < N:
                value = value + g[mate][half]
            value = s_ref[v, at, :] + value
            if source is not None:
                value = value + source(at)
            if inner:
                out_ref[at, :] = value
            else:
                out_ref[v, at, :] = value


def start_body(s_ref, g_ref, from_left, from_right, top_ref, bottom_ref, out_ref):
    rows_body(NV, g_ref, from_left, from_right, top_ref, bottom_ref)
    low, high = ends()

    def one(v, carry):
        advance(s_ref, g_ref, from_left, from_right, v, low, high, None, out_ref)
        return carry

    lax.fori_loop(0, NV, one, 0)


def update_body(
    s_ref, g_ref, from_left, from_right, raw_ref, sum_ref, out_ref, pass_ref
):
    pass_ref[...] = sum_ref[...]
    low, high = ends()

    def one(v, carry):
        advance(
            s_ref, g_ref, from_left, from_right, v, low, high,
            lambda at: STEP * raw_ref[v, at, :], out_ref,
        )
        return carry

    lax.fori_loop(0, NV, one, 0)
    advance(s_ref, g_ref, from_left, from_right, NV, low, high, lambda at: STEP, out_ref)


def edges_body(s_ref, above_ref, below_ref, edge_ref, out_ref, left_ref, right_ref):
    def one(v, carry):
        out_ref[v, 0:16, :] = s_ref[v, 0:16, :] + above_ref[v]
        out_ref[v, 16:240, :] = s_ref[v, 16:240, :]
        out_ref[v, 240:256, :] = s_ref[v, 240:256, :] + below_ref[v]
        return carry

    lax.fori_loop(0, NV, one, 0)
    if above_ref.shape[0] == NF:
        one(NV, 0)
    else:
        out_ref[NV] = s_ref[NV]
    write_edges(NF, out_ref, edge_ref, left_ref, right_ref)


def output_body(
    columns, s_ref, g_ref, from_left, from_right, raw_ref, sum_ref, more_ref,
    new_hbm, tend_hbm, top_ref, bottom_ref, new_ref, tend_ref, response, sems,
):
    low, high = ends()
    copies = []
    for v in range(NV):
        copies.append(pltpu.make_async_copy(tend_ref.at[v], tend_hbm.at[v], sems.at[0, v]))
        copies.append(pltpu.make_async_copy(new_ref.at[v], new_hbm.at[v], sems.at[1, v]))
    advance(s_ref, g_ref, from_left, from_right, NV, low, high, lambda at: STEP, response, True)
    for v in range(NV):
        mean = (sum_ref[v : v + 1, :] + more_ref[v : v + 1, :]) * (1.0 / columns)
        tend_ref[v] = raw_ref[v] - mean
        copies[2 * v].start()
    for v in range(NV):
        mean = (sum_ref[v : v + 1, :] + more_ref[v : v + 1, :]) * (1.0 / columns)
        advance(
            s_ref, g_ref, from_left, from_right, v, low, high,
            lambda at: STEP * raw_ref[v, at, :] - mean * response[at, :], new_ref.at[v], True,
        )
        copies[2 * v + 1].start()
        top_ref[v] = new_ref[v, 0:16, :]
        bottom_ref[v] = new_ref[v, 240:256, :]
    for copy in copies:
        copy.wait()


def output(columns, s, g, from_left, from_right, raw, total, more):
    anywhere = pl.BlockSpec(memory_space=pltpu.HBM)
    return pl.pallas_call(
      functools.partial(output_body, columns),
      out_shape=(jax.ShapeDtypeStruct((NV, 256, LEV), F32),) * 2
      + (jax.ShapeDtypeStruct((NV, N, LEV), F32),) * 2,
      in_specs=[vmem()] * 7,
      out_specs=(anywhere, anywhere, vmem(), vmem()),
      scratch_shapes=[
          pltpu.VMEM((NV, 256, LEV), F32), pltpu.VMEM((NV, 256, LEV), F32),
          pltpu.VMEM((256, LEV), F32), pltpu.SemaphoreType.DMA((2, NV)),
      ],
      compiler_params=pltpu.CompilerParams(vmem_limit_bytes=8 << 20),
      cost_estimate=pl.CostEstimate(flops=10**7, bytes_accessed=8 * 10**6, transcendentals=0),
      name="output",
    )(s, g, from_left, from_right, raw, total, more)


def patch_body(
    columns, part_ref, top_ref, bottom_ref, above_ref, below_ref, sum_ref, more_ref,
    new_ref, rows_ref, sems,
):
    for v in range(NV):
        mean = (sum_ref[pl.ds(v, 1), :] + more_ref[pl.ds(v, 1), :]) * (1.0 / columns)
        rows_ref[0, v] = top_ref[v] + above_ref[v] - mean * above_ref[NV]
        rows_ref[1, v] = bottom_ref[v] + below_ref[v] - mean * below_ref[NV]
    copies = [
        pltpu.make_async_copy(rows_ref.at[0], new_ref.at[:, 0:16, :], sems.at[0]),
        pltpu.make_async_copy(rows_ref.at[1], new_ref.at[:, 240:256, :], sems.at[1]),
    ]
    for copy in copies:
        copy.start()
    for copy in copies:
        copy.wait()


def patch(columns, part, top, bottom, above, below, total, more):
    anywhere = pl.BlockSpec(memory_space=pltpu.HBM)
    return pl.pallas_call(
        functools.partial(patch_body, columns),
        out_shape=jax.ShapeDtypeStruct((NV, 256, LEV), F32),
        in_specs=[anywhere] + [vmem()] * 6,
        out_specs=anywhere,
        scratch_shapes=[pltpu.VMEM((2, NV, N, LEV), F32), pltpu.SemaphoreType.DMA((2,))],
        input_output_aliases={0: 0},
        compiler_params=pltpu.CompilerParams(vmem_limit_bytes=6 << 20),
        cost_estimate=pl.CostEstimate(flops=10**6, bytes_accessed=10**6, transcendentals=0),
        name="patch",
    )(part, top, bottom, above, below, total, more)


def shifted(value, axis, by):
    count = lax.axis_size(axis)
    return lax.ppermute(value, axis, [(i, (i + by) % count) for i in range(count)])


def partner(value, axis, bit):
    count = lax.axis_size(axis)
    return lax.ppermute(value, axis, [(i, i ^ bit) for i in range(count)])


def exchanged(low, high, axis):
    from_low = shifted(high, axis, 1)
    return from_low, shifted(low, axis, -1)


def per_device(state, wind_x, wind_y, level_mix, field_mix, block_cost):
    state = state.reshape(NV, 256, LEV)
    wind_x = wind_x.reshape(256, LEV)
    wind_y = wind_y.reshape(256, LEV)
    slab = (256, LEV)
    edge12, edge13 = (NV, N, LEV), (NF, N, LEV)
    state, wxs, wys, edge, left, right = call(
        first_body,
        tuple(pltpu.with_memory_space_constraint(x, pltpu.HBM) for x in (state, wind_x, wind_y)),
        ((NV, 256, LEV), slab, slab, (2, 5, N, LEV), edge12, edge12), 1, hbm=3,
        scratch=(
            pltpu.VMEM(slab, BF16), pltpu.VMEM(slab, BF16), pltpu.SemaphoreType.DMA((NV + 2,)),
        ),
    )
    from_left, from_right = exchanged(left, right, "narrow")
    (g,) = call(functools.partial(full_body, NV), (state, wxs, wys), ((NV, 256, LEV),), 3)
    top, bottom, moved = call(
        start_body, (state, g, from_left, from_right),
        (edge12, edge12, (NV, 256, LEV)), 0.6,
    )
    above, below = exchanged(top, bottom, "wide")
    raw, total, s = call(
        physics_body, (block_cost, state, level_mix, field_mix, moved),
        ((NV, 256, LEV), (NV, LEV), (NF, 256, LEV)), 20,
        scratch=(pltpu.VMEM((96, 256), BF16), pltpu.VMEM((256, 256), BF16)), smem=1,
    )
    more = partner(total, "wide", 8)
    plan = [
        [("wide", 4)], [("narrow", 1), ("narrow", 2), ("narrow", 3)],
        [("wide", 2)], [("wide", 1)], [("narrow", 4)],
    ]
    window = 0

    def next_sum(passed, more):
        nonlocal window
        total = passed + more
        if window < len(plan):
            parts = []
            for step in plan[window]:
                parts.append(partner(total, *step))
            more = functools.reduce(jnp.add, parts)
        window += 1
        return total, more

    columns = 256 * lax.axis_size("wide") * lax.axis_size("narrow")
    for k in range(1, NSUB):
        s, left, right = call(
            edges_body, (s, above, below, edge),
            ((NF, 256, LEV), edge13, edge13), 0.7,
        )
        from_left, from_right = exchanged(left, right, "narrow")
        g, total = call(
            functools.partial(full_body, NF), (s, wxs, wys, total),
            ((NF, 256, LEV), (NV, LEV)), 3,
        )
        total, more = next_sum(total, more)
        top, bottom = call(
            functools.partial(rows_body, NF), (g, from_left, from_right),
            (edge13, edge13), 0.3,
        )
        above, below = exchanged(top, bottom, "wide")
        if k < NSUB - 1:
            s, total = call(
                update_body, (s, g, from_left, from_right, raw, total),
                ((NF, 256, LEV), (NV, LEV)), 1,
            )
            total, more = next_sum(total, more)
    part, tendency, top, bottom = output(
        columns, s, g, from_left, from_right, raw, total, more
    )
    new_state = patch(columns, part, top, bottom, above, below, total, more)
    return new_state.reshape(NV, N, N, LEV), tendency.reshape(NV, N, N, LEV)


def solution(mesh):
    placed = (
        P(None, "wide", "narrow", None),
        P("wide", "narrow", None),
        P("wide", "narrow", None),
        P(),
        P(),
        P("wide", "narrow"),
    )
    return jax.shard_map(
        per_device,
        mesh=mesh,
        in_specs=placed,
        out_specs=(P(None, "wide", "narrow", None), P(None, "wide", "narrow", None)),
        check_vma=False,
    )
```

profile of v0, /device:TPU:0, one launch (start us, length us, event | category | flops | bytes accessed | tf_op | source)
XLA Modules:
  0.0 96.7 jit_solution(18040192865812327153)
XLA Ops:
  0.6 2.0 %shard_map.77 = (f32[12,256,128]{2,1,0:T(8,128)S(1)}, f32[256,128]{1,0:T(8,128)S(1)}, f32[256,128]{1,0:T(8,128)S(1)}, f32[2,5,16,128]{3,2,1,0:T(8,128)S(1)}, f32...) custom-call(f32[12,256,128]{2,1,0:T(8,128)} %bitcast.6, bf16[256,128]{1,0:T(8,128)(2,1)} %bitcast.7, ...), custom_call_target="tpu_custom_call" | custom-call | flops 4000000 | bytes 2000000 | tf_op jit(solution)/shard_map/pallas_call | solution.py:45
  2.6 2.9 %collective-permute-start.1 = (f32[12,16,128]{2,1,0:T(8,128)S(1)}, f32[12,16,128]{2,1,0:T(8,128)S(1)}, u32[]{:S(2)}, u32[]{:S(2)}) collective-permute-start(f32[12,16,128]{2,1,0:T(8,128)S(1)} %get-tuple-element.47), channel_id=1, source_target_pairs={{0,7},{1,0},{2,1},{3,2},{4,3},{5,4},{6,5},{7,6},{8,15},{9,8},{10,9... | collective-permute-start | bytes 294920 | tf_op jit(solution)/shard_map/ppermute | solution.py:444
  8.9 1.6 %collective-permute-start.2 = (f32[12,16,128]{2,1,0:T(8,128)}, f32[12,16,128]{2,1,0:T(8,128)}, u32[]{:S(2)}, u32[]{:S(2)}) collective-permute-start(f32[12,16,128]{2,1,0:T(8,128)} %get-tuple-element.50), channel_id=1, source_target_pairs={{0,8},{8,16},{16,24},{24,32},{32,40},{40,48},{48,56},{56,64},{64,7... | collective-permute-start | bytes 294920 | tf_op jit(solution)/shard_map/ppermute | solution.py:444
  10.5 4.7 %collective-permute-start.3 = (f32[12,16,128]{2,1,0:T(8,128)}, f32[12,16,128]{2,1,0:T(8,128)}, u32[]{:S(2)}, u32[]{:S(2)}) collective-permute-start(f32[12,16,128]{2,1,0:T(8,128)} %get-tuple-element.51), channel_id=1, source_target_pairs={{0,120},{8,0},{16,8},{24,16},{32,24},{40,32},{48,40},{56,48},{64,5... | collective-permute-start | bytes 294920 | tf_op jit(solution)/shard_map/ppermute | solution.py:444
  15.4 6.4 %shard_map.80 = (f32[12,256,128]{2,1,0:T(8,128)S(1)}, f32[12,128]{1,0:T(8,128)S(1)}, f32[13,256,128]{2,1,0:T(8,128)S(1)}) custom-call(s32[2,1]{1,0:T(2,128)S(1)} %copy.9.count_ref, f32[12,256,128]{2,1,0:T(8,128)S(1)} %get-tuple-element.43.s_ref.state_ref, bf16[128,128]{1,0:T(8,128)(2,1)S(1)} %copy-done, f32[12,12]{1,0:T(8,128)S(1)} %copy-done.1, ...), custom_call_target="tpu_custom_call" | custom-call | flops 80000000 | bytes 40000000 | tf_op jit(solution)/shard_map/pallas_call | solution.py:45
  21.8 1.5 %shard_map.81 = (f32[13,256,128]{2,1,0:T(8,128)S(1)}, f32[13,16,128]{2,1,0:T(8,128)S(1)}, f32[13,16,128]{2,1,0:T(8,128)S(1)}) custom-call(f32[13,256,128]{2,1,0:T(8,128)S(1)} %get-tuple-element.49.s_ref, f32[12,16,128]{2,1,0:T(8,128)} %collective-permute-done.2.above_ref, f32[12,16,128]{2,1,0:T(8,128)} %collective-permute-done.3.below_ref, ...), custom_call_target="tpu_custom_call" | custom-call | flops 2800000 | bytes 1400000 | tf_op jit(solution)/shard_map/pallas_call | solution.py:45
  24.0 3.1 %collective-permute-start.5 = (f32[13,16,128]{2,1,0:T(8,128)S(1)}, f32[13,16,128]{2,1,0:T(8,128)S(1)}, u32[]{:S(2)}, u32[]{:S(2)}) collective-permute-start(f32[13,16,128]{2,1,0:T(8,128)S(1)} %get-tuple-element.57), channel_id=1, source_target_pairs={{0,7},{1,0},{2,1},{3,2},{4,3},{5,4},{6,5},{7,6},{8,15},{9,8},{10,9... | collective-permute-start | bytes 319496 | tf_op jit(solution)/shard_map/ppermute | solution.py:444
  27.1 1.3 %shard_map.82 = (f32[13,256,128]{2,1,0:T(8,128)S(1)}, f32[12,128]{1,0:T(8,128)S(1)}) custom-call(f32[13,256,128]{2,1,0:T(8,128)S(1)} %get-tuple-element.53.s_ref, f32[256,128]{1,0:T(8,128)S(1)} %get-tuple-element.44.wxs_ref, f32[256,128]{1,0:T(8,128)S(1)} %get-tuple-element.45.wys_ref, f32[12,128]{1,0:T(8,128)S(1)} %get-tuple-element.54.refs_0_), custom_call_target="tpu_custom_call" | custom-call | flops 12000000 | bytes 6000000 | tf_op jit(solution)/shard_map/pallas_call | solution.py:45
  29.6 5.3 %collective-permute-start.8 = (f32[13,16,128]{2,1,0:T(8,128)S(1)}, f32[13,16,128]{2,1,0:T(8,128)S(1)}, u32[]{:S(2)}, u32[]{:S(2)}) collective-permute-start(f32[13,16,128]{2,1,0:T(8,128)S(1)} %get-tuple-element.62), channel_id=1, source_target_pairs={{0,120},{8,0},{16,8},{24,16},{32,24},{40,32},{48,40},{56,48},{64,5... | collective-permute-start | bytes 319496 | tf_op jit(solution)/shard_map/ppermute | solution.py:444
  35.0 13.9 %collective-permute-start.6 = (f32[12,128]{1,0:T(8,128)S(1)}, f32[12,128]{1,0:T(8,128)S(1)}, u32[]{:S(2)}, u32[]{:S(2)}) collective-permute-start(f32[12,128]{1,0:T(8,128)S(1)} %get-tuple-element.54.refs_0_), channel_id=1, source_target_pairs={{0,64},{8,72},{16,80},{24,88},{32,96},{40,104},{48,112},{56,120},{... | collective-permute-start | bytes 18440 | tf_op jit(solution)/shard_map/ppermute | solution.py:449
  48.8 1.6 %collective-permute-done.6 = f32[12,128]{1,0:T(8,128)S(1)} collective-permute-done((f32[12,128]{1,0:T(8,128)S(1)}, f32[12,128]{1,0:T(8,128)S(1)}, u32[]{:S(2)}, u32[]{:S(2)}) %collective-permute-start.6) | collective-permute-done | bytes 6176 | tf_op jit(solution)/shard_map/ppermute | solution.py:449
  51.6 2.9 %collective-permute-start.11 = (f32[13,16,128]{2,1,0:T(8,128)S(1)}, f32[13,16,128]{2,1,0:T(8,128)S(1)}, u32[]{:S(2)}, u32[]{:S(2)}) collective-permute-start(f32[13,16,128]{2,1,0:T(8,128)S(1)} %get-tuple-element.67), channel_id=1, source_target_pairs={{0,7},{1,0},{2,1},{3,2},{4,3},{5,4},{6,5},{7,6},{8,15},{9,8},{10,9... | collective-permute-start | bytes 319496 | tf_op jit(solution)/shard_map/ppermute | solution.py:444
  54.5 3.6 %collective-permute-done.9 = f32[12,128]{1,0:T(8,128)S(1)} collective-permute-done((f32[12,128]{1,0:T(8,128)S(1)}, f32[12,128]{1,0:T(8,128)S(1)}, u32[]{:S(2)}, u32[]{:S(2)}) %collective-permute-start.9) | collective-permute-done | bytes 6176 | tf_op jit(solution)/shard_map/ppermute | solution.py:449
  58.2 1.9 %collective-permute-start.12 = (f32[12,128]{1,0:T(8,128)S(1)}, f32[12,128]{1,0:T(8,128)S(1)}, u32[]{:S(2)}, u32[]{:S(2)}) collective-permute-start(f32[12,128]{1,0:T(8,128)S(1)} %add.22.refs_0_), channel_id=1, source_target_pairs={{0,1},{1,0},{2,3},{3,2},{4,5},{5,4},{6,7},{7,6},{8,9},{9,8},{10,11... | collective-permute-start | bytes 18440 | tf_op jit(solution)/shard_map/ppermute | solution.py:449
  60.0 1.3 %shard_map.86 = (f32[13,256,128]{2,1,0:T(8,128)S(1)}, f32[12,128]{1,0:T(8,128)S(1)}) custom-call(f32[13,256,128]{2,1,0:T(8,128)S(1)} %get-tuple-element.63.s_ref, f32[256,128]{1,0:T(8,128)S(1)} %get-tuple-element.44.wxs_ref, f32[256,128]{1,0:T(8,128)S(1)} %get-tuple-element.45.wys_ref, f32[12,128]{1,0:T(8,128)S(1)} %add.22.refs_0_), custom_call_target="tpu_custom_call" | custom-call | flops 12000000 | bytes 6000000 | tf_op jit(solution)/shard_map/pallas_call | solution.py:45
  61.5 5.3 %collective-permute-start.16 = (f32[13,16,128]{2,1,0:T(8,128)S(1)}, f32[13,16,128]{2,1,0:T(8,128)S(1)}, u32[]{:S(2)}, u32[]{:S(2)}) collective-permute-start(f32[13,16,128]{2,1,0:T(8,128)S(1)} %get-tuple-element.71), channel_id=1, source_target_pairs={{0,120},{8,0},{16,8},{24,16},{32,24},{40,32},{48,40},{56,48},{64,5... | collective-permute-start | bytes 319496 | tf_op jit(solution)/shard_map/ppermute | solution.py:444
  67.4 2.3 %collective-permute-done.15.above_ref = f32[13,16,128]{2,1,0:T(8,128)S(1)} collective-permute-done((f32[13,16,128]{2,1,0:T(8,128)S(1)}, f32[13,16,128]{2,1,0:T(8,128)S(1)}, u32[]{:S(2)}, u32[]{:S(2)}) %collective-permute-start.15) | collective-permute-done | bytes 106528 | tf_op jit(solution)/shard_map/ppermute | solution.py:444
  70.3 2.9 %collective-permute-start.19 = (f32[13,16,128]{2,1,0:T(8,128)S(1)}, f32[13,16,128]{2,1,0:T(8,128)S(1)}, u32[]{:S(2)}, u32[]{:S(2)}) collective-permute-start(f32[13,16,128]{2,1,0:T(8,128)S(1)} %get-tuple-element.76), channel_id=1, source_target_pairs={{0,7},{1,0},{2,1},{3,2},{4,3},{5,4},{6,5},{7,6},{8,15},{9,8},{10,9... | collective-permute-start | bytes 319496 | tf_op jit(solution)/shard_map/ppermute | solution.py:444
  73.2 5.2 %collective-permute-done.17 = f32[12,128]{1,0:T(8,128)S(1)} collective-permute-done((f32[12,128]{1,0:T(8,128)S(1)}, f32[12,128]{1,0:T(8,128)S(1)}, u32[]{:S(2)}, u32[]{:S(2)}) %collective-permute-start.17) | collective-permute-done | bytes 6176 | tf_op jit(solution)/shard_map/ppermute | solution.py:449
  78.4 1.3 %shard_map.90 = (f32[13,256,128]{2,1,0:T(8,128)S(1)}, f32[12,128]{1,0:T(8,128)S(1)}) custom-call(f32[13,256,128]{2,1,0:T(8,128)S(1)} %get-tuple-element.72.s_ref, f32[256,128]{1,0:T(8,128)S(1)} %get-tuple-element.44.wxs_ref, f32[256,128]{1,0:T(8,128)S(1)} %get-tuple-element.45.wys_ref, f32[12,128]{1,0:T(8,128)S(1)} %add.26.refs_0_), custom_call_target="tpu_custom_call" | custom-call | flops 12000000 | bytes 6000000 | tf_op jit(solution)/shard_map/pallas_call | solution.py:45
  79.9 5.3 %collective-permute-start.23 = (f32[13,16,128]{2,1,0:T(8,128)S(1)}, f32[13,16,128]{2,1,0:T(8,128)S(1)}, u32[]{:S(2)}, u32[]{:S(2)}) collective-permute-start(f32[13,16,128]{2,1,0:T(8,128)S(1)} %get-tuple-element.82), channel_id=1, source_target_pairs={{0,120},{8,0},{16,8},{24,16},{32,24},{40,32},{48,40},{56,48},{64,5... | collective-permute-start | bytes 319496 | tf_op jit(solution)/shard_map/ppermute | solution.py:444
  85.2 3.6 %collective-permute-done.20 = f32[12,128]{1,0:T(8,128)S(1)} collective-permute-done((f32[12,128]{1,0:T(8,128)S(1)}, f32[12,128]{1,0:T(8,128)S(1)}, u32[]{:S(2)}, u32[]{:S(2)}) %collective-permute-start.20) | collective-permute-done | bytes 6176 | tf_op jit(solution)/shard_map/ppermute | solution.py:449
  88.9 5.2 %collective-permute-done.21.more_ref = f32[12,128]{1,0:T(8,128)S(1)} collective-permute-done((f32[12,128]{1,0:T(8,128)S(1)}, f32[12,128]{1,0:T(8,128)S(1)}, u32[]{:S(2)}, u32[]{:S(2)}) %collective-permute-start.21) | collective-permute-done | bytes 6176 | tf_op jit(solution)/shard_map/ppermute | solution.py:449
  94.0 1.9 %output.1 = (f32[12,256,128]{2,1,0:T(8,128)}, f32[12,256,128]{2,1,0:T(8,128)}, f32[12,16,128]{2,1,0:T(8,128)S(1)}, f32[12,16,128]{2,1,0:T(8,128)S(1)}) custom-call(f32[13,256,128]{2,1,0:T(8,128)S(1)} %get-tuple-element.72.s_ref, f32[13,256,128]{2,1,0:T(8,128)S(1)} %get-tuple-element.74.g_ref, f32[13,16,128]{2,1,0:T(8,128)S(1)} %collective-permute-done.18.from_left, ...), custom_call_target="tpu_custom_call" | custom-call | flops 10000000 | bytes 8000000 | tf_op jit(solution)/shard_map/output/pallas_call | solution.py:393
  (53 shorter events, 8.7 us)
Async XLA Ops:
  2.6 5.3 %collective-permute-start = (f32[12,16,128]{2,1,0:T(8,128)S(1)}, f32[12,16,128]{2,1,0:T(8,128)S(1)}, u32[]{:S(2)}, u32[]{:S(2)}) collective-permute-start(f32[12,16,128]{2,1,0:T(8,128)S(1)} %get-tuple-element.46), channel_id=1, source_target_pairs={{0,1},{1,2},{2,3},{3,4},{4,5},{5,6},{6,7},{7,0},{8,9},{9,10},{10,1... | collective-permute-start | bytes 294920 | tf_op jit(solution)/shard_map/ppermute | solution.py:444
  2.6 5.2 %collective-permute-start.1 = (f32[12,16,128]{2,1,0:T(8,128)S(1)}, f32[12,16,128]{2,1,0:T(8,128)S(1)}, u32[]{:S(2)}, u32[]{:S(2)}) collective-permute-start(f32[12,16,128]{2,1,0:T(8,128)S(1)} %get-tuple-element.47), channel_id=1, source_target_pairs={{0,7},{1,0},{2,1},{3,2},{4,3},{5,4},{6,5},{7,6},{8,15},{9,8},{10,9... | collective-permute-start | bytes 294920 | tf_op jit(solution)/shard_map/ppermute | solution.py:444
  8.9 12.8 %collective-permute-start.2 = (f32[12,16,128]{2,1,0:T(8,128)}, f32[12,16,128]{2,1,0:T(8,128)}, u32[]{:S(2)}, u32[]{:S(2)}) collective-permute-start(f32[12,16,128]{2,1,0:T(8,128)} %get-tuple-element.50), channel_id=1, source_target_pairs={{0,8},{8,16},{16,24},{24,32},{32,40},{40,48},{48,56},{56,64},{64,7... | collective-permute-start | bytes 294920 | tf_op jit(solution)/shard_map/ppermute | solution.py:444
  10.5 11.2 %collective-permute-start.3 = (f32[12,16,128]{2,1,0:T(8,128)}, f32[12,16,128]{2,1,0:T(8,128)}, u32[]{:S(2)}, u32[]{:S(2)}) collective-permute-start(f32[12,16,128]{2,1,0:T(8,128)} %get-tuple-element.51), channel_id=1, source_target_pairs={{0,120},{8,0},{16,8},{24,16},{32,24},{40,32},{48,40},{56,48},{64,5... | collective-permute-start | bytes 294920 | tf_op jit(solution)/shard_map/ppermute | solution.py:444
  23.3 6.2 %collective-permute-start.4 = (f32[13,16,128]{2,1,0:T(8,128)S(1)}, f32[13,16,128]{2,1,0:T(8,128)S(1)}, u32[]{:S(2)}, u32[]{:S(2)}) collective-permute-start(f32[13,16,128]{2,1,0:T(8,128)S(1)} %get-tuple-element.56), channel_id=1, source_target_pairs={{0,1},{1,2},{2,3},{3,4},{4,5},{5,6},{6,7},{7,0},{8,9},{9,10},{10,1... | collective-permute-start | bytes 319496 | tf_op jit(solution)/shard_map/ppermute | solution.py:444
  24.0 5.4 %collective-permute-start.5 = (f32[13,16,128]{2,1,0:T(8,128)S(1)}, f32[13,16,128]{2,1,0:T(8,128)S(1)}, u32[]{:S(2)}, u32[]{:S(2)}) collective-permute-start(f32[13,16,128]{2,1,0:T(8,128)S(1)} %get-tuple-element.57), channel_id=1, source_target_pairs={{0,7},{1,0},{2,1},{3,2},{4,3},{5,4},{6,5},{7,6},{8,15},{9,8},{10,9... | collective-permute-start | bytes 319496 | tf_op jit(solution)/shard_map/ppermute | solution.py:444
  29.5 21.4 %collective-permute-start.7 = (f32[13,16,128]{2,1,0:T(8,128)S(1)}, f32[13,16,128]{2,1,0:T(8,128)S(1)}, u32[]{:S(2)}, u32[]{:S(2)}) collective-permute-start(f32[13,16,128]{2,1,0:T(8,128)S(1)} %get-tuple-element.61), channel_id=1, source_target_pairs={{0,8},{8,16},{16,24},{24,32},{32,40},{40,48},{48,56},{56,64},{64,7... | collective-permute-start | bytes 319496 | tf_op jit(solution)/shard_map/ppermute | solution.py:444
  29.6 21.3 %collective-permute-start.8 = (f32[13,16,128]{2,1,0:T(8,128)S(1)}, f32[13,16,128]{2,1,0:T(8,128)S(1)}, u32[]{:S(2)}, u32[]{:S(2)}) collective-permute-start(f32[13,16,128]{2,1,0:T(8,128)S(1)} %get-tuple-element.62), channel_id=1, source_target_pairs={{0,120},{8,0},{16,8},{24,16},{32,24},{40,32},{48,40},{56,48},{64,5... | collective-permute-start | bytes 319496 | tf_op jit(solution)/shard_map/ppermute | solution.py:444
  35.0 15.5 %collective-permute-start.6 = (f32[12,128]{1,0:T(8,128)S(1)}, f32[12,128]{1,0:T(8,128)S(1)}, u32[]{:S(2)}, u32[]{:S(2)}) collective-permute-start(f32[12,128]{1,0:T(8,128)S(1)} %get-tuple-element.54.refs_0_), channel_id=1, source_target_pairs={{0,64},{8,72},{16,80},{24,88},{32,96},{40,104},{48,112},{56,120},{... | collective-permute-start | bytes 18440 | tf_op jit(solution)/shard_map/ppermute | solution.py:449
  51.5 9.8 %collective-permute-start.10 = (f32[13,16,128]{2,1,0:T(8,128)S(1)}, f32[13,16,128]{2,1,0:T(8,128)S(1)}, u32[]{:S(2)}, u32[]{:S(2)}) collective-permute-start(f32[13,16,128]{2,1,0:T(8,128)S(1)} %get-tuple-element.66), channel_id=1, source_target_pairs={{0,1},{1,2},{2,3},{3,4},{4,5},{5,6},{6,7},{7,0},{8,9},{9,10},{10,1... | collective-permute-start | bytes 319496 | tf_op jit(solution)/shard_map/ppermute | solution.py:444
  51.6 9.8 %collective-permute-start.11 = (f32[13,16,128]{2,1,0:T(8,128)S(1)}, f32[13,16,128]{2,1,0:T(8,128)S(1)}, u32[]{:S(2)}, u32[]{:S(2)}) collective-permute-start(f32[13,16,128]{2,1,0:T(8,128)S(1)} %get-tuple-element.67), channel_id=1, source_target_pairs={{0,7},{1,0},{2,1},{3,2},{4,3},{5,4},{6,5},{7,6},{8,15},{9,8},{10,9... | collective-permute-start | bytes 319496 | tf_op jit(solution)/shard_map/ppermute | solution.py:444
  54.5 3.7 %collective-permute-start.9 = (f32[12,128]{1,0:T(8,128)S(1)}, f32[12,128]{1,0:T(8,128)S(1)}, u32[]{:S(2)}, u32[]{:S(2)}) collective-permute-start(f32[12,128]{1,0:T(8,128)S(1)} %add.21.sum_ref), channel_id=1, source_target_pairs={{0,32},{8,40},{16,48},{24,56},{32,0},{40,8},{48,16},{56,24},{64,96... | collective-permute-start | bytes 18440 | tf_op jit(solution)/shard_map/ppermute | solution.py:449
  58.2 8.7 %collective-permute-start.14 = (f32[12,128]{1,0:T(8,128)S(1)}, f32[12,128]{1,0:T(8,128)S(1)}, u32[]{:S(2)}, u32[]{:S(2)}) collective-permute-start(f32[12,128]{1,0:T(8,128)S(1)} %add.22.refs_0_), channel_id=1, source_target_pairs={{0,3},{1,2},{2,1},{3,0},{4,7},{5,6},{6,5},{7,4},{8,11},{9,10},{10,... | collective-permute-start | bytes 18440 | tf_op jit(solution)/shard_map/ppermute | solution.py:449
  58.2 8.7 %collective-permute-start.13 = (f32[12,128]{1,0:T(8,128)S(1)}, f32[12,128]{1,0:T(8,128)S(1)}, u32[]{:S(2)}, u32[]{:S(2)}) collective-permute-start(f32[12,128]{1,0:T(8,128)S(1)} %add.22.refs_0_), channel_id=1, source_target_pairs={{0,2},{1,3},{2,0},{3,1},{4,6},{5,7},{6,4},{7,5},{8,10},{9,11},{10,... | collective-permute-start | bytes 18440 | tf_op jit(solution)/shard_map/ppermute | solution.py:449
  58.2 8.7 %collective-permute-start.12 = (f32[12,128]{1,0:T(8,128)S(1)}, f32[12,128]{1,0:T(8,128)S(1)}, u32[]{:S(2)}, u32[]{:S(2)}) collective-permute-start(f32[12,128]{1,0:T(8,128)S(1)} %add.22.refs_0_), channel_id=1, source_target_pairs={{0,1},{1,0},{2,3},{3,2},{4,5},{5,4},{6,7},{7,6},{8,9},{9,8},{10,11... | collective-permute-start | bytes 18440 | tf_op jit(solution)/shard_map/ppermute | solution.py:449
  61.4 8.3 %collective-permute-start.15 = (f32[13,16,128]{2,1,0:T(8,128)S(1)}, f32[13,16,128]{2,1,0:T(8,128)S(1)}, u32[]{:S(2)}, u32[]{:S(2)}) collective-permute-start(f32[13,16,128]{2,1,0:T(8,128)S(1)} %get-tuple-element.70), channel_id=1, source_target_pairs={{0,8},{8,16},{16,24},{24,32},{32,40},{40,48},{48,56},{56,64},{64,7... | collective-permute-start | bytes 319496 | tf_op jit(solution)/shard_map/ppermute | solution.py:444
  61.5 8.2 %collective-permute-start.16 = (f32[13,16,128]{2,1,0:T(8,128)S(1)}, f32[13,16,128]{2,1,0:T(8,128)S(1)}, u32[]{:S(2)}, u32[]{:S(2)}) collective-permute-start(f32[13,16,128]{2,1,0:T(8,128)S(1)} %get-tuple-element.71), channel_id=1, source_target_pairs={{0,120},{8,0},{16,8},{24,16},{32,24},{40,32},{48,40},{56,48},{64,5... | collective-permute-start | bytes 319496 | tf_op jit(solution)/shard_map/ppermute | solution.py:444
  70.3 9.4 %collective-permute-start.18 = (f32[13,16,128]{2,1,0:T(8,128)S(1)}, f32[13,16,128]{2,1,0:T(8,128)S(1)}, u32[]{:S(2)}, u32[]{:S(2)}) collective-permute-start(f32[13,16,128]{2,1,0:T(8,128)S(1)} %get-tuple-element.75), channel_id=1, source_target_pairs={{0,1},{1,2},{2,3},{3,4},{4,5},{5,6},{6,7},{7,0},{8,9},{9,10},{10,1... | collective-permute-start | bytes 319496 | tf_op jit(solution)/shard_map/ppermute | solution.py:444
  70.3 9.4 %collective-permute-start.19 = (f32[13,16,128]{2,1,0:T(8,128)S(1)}, f32[13,16,128]{2,1,0:T(8,128)S(1)}, u32[]{:S(2)}, u32[]{:S(2)}) collective-permute-start(f32[13,16,128]{2,1,0:T(8,128)S(1)} %get-tuple-element.76), channel_id=1, source_target_pairs={{0,7},{1,0},{2,1},{3,2},{4,3},{5,4},{6,5},{7,6},{8,15},{9,8},{10,9... | collective-permute-start | bytes 319496 | tf_op jit(solution)/shard_map/ppermute | solution.py:444
  73.2 5.2 %collective-permute-start.17 = (f32[12,128]{1,0:T(8,128)S(1)}, f32[12,128]{1,0:T(8,128)S(1)}, u32[]{:S(2)}, u32[]{:S(2)}) collective-permute-start(f32[12,128]{1,0:T(8,128)S(1)} %add_add_fusion.sum_ref), channel_id=1, source_target_pairs={{0,16},{8,24},{16,0},{24,8},{32,48},{40,56},{48,32},{56,40},{64,80... | collective-permute-start | bytes 18440 | tf_op jit(solution)/shard_map/ppermute | solution.py:449
  79.8 16.1 %collective-permute-start.22 = (f32[13,16,128]{2,1,0:T(8,128)S(1)}, f32[13,16,128]{2,1,0:T(8,128)S(1)}, u32[]{:S(2)}, u32[]{:S(2)}) collective-permute-start(f32[13,16,128]{2,1,0:T(8,128)S(1)} %get-tuple-element.81), channel_id=1, source_target_pairs={{0,8},{8,16},{16,24},{24,32},{32,40},{40,48},{48,56},{56,64},{64,7... | collective-permute-start | bytes 319496 | tf_op jit(solution)/shard_map/ppermute | solution.py:444
  79.9 16.0 %collective-permute-start.23 = (f32[13,16,128]{2,1,0:T(8,128)S(1)}, f32[13,16,128]{2,1,0:T(8,128)S(1)}, u32[]{:S(2)}, u32[]{:S(2)}) collective-permute-start(f32[13,16,128]{2,1,0:T(8,128)S(1)} %get-tuple-element.82), channel_id=1, source_target_pairs={{0,120},{8,0},{16,8},{24,16},{32,24},{40,32},{48,40},{56,48},{64,5... | collective-permute-start | bytes 319496 | tf_op jit(solution)/shard_map/ppermute | solution.py:444
  85.2 3.7 %collective-permute-start.20 = (f32[12,128]{1,0:T(8,128)S(1)}, f32[12,128]{1,0:T(8,128)S(1)}, u32[]{:S(2)}, u32[]{:S(2)}) collective-permute-start(f32[12,128]{1,0:T(8,128)S(1)} %add.26.refs_0_), channel_id=1, source_target_pairs={{0,8},{8,0},{16,24},{24,16},{32,40},{40,32},{48,56},{56,48},{64,72... | collective-permute-start | bytes 18440 | tf_op jit(solution)/shard_map/ppermute | solution.py:449
  88.9 5.2 %collective-permute-start.21 = (f32[12,128]{1,0:T(8,128)S(1)}, f32[12,128]{1,0:T(8,128)S(1)}, u32[]{:S(2)}, u32[]{:S(2)}) collective-permute-start(f32[12,128]{1,0:T(8,128)S(1)} %add.27.sum_ref), channel_id=1, source_target_pairs={{0,4},{1,5},{2,6},{3,7},{4,0},{5,1},{6,2},{7,3},{8,12},{9,13},{10,... | collective-permute-start | bytes 18440 | tf_op jit(solution)/shard_map/ppermute | solution.py:449
  (3 other events, 25.7 us)
where the time goes:
time: 96.8 us; the launch traced here: 96.7 us
  starting transfers between devices  51 us (53%)
  waiting for transfers between devices  23.8 us (25%)
  Pallas kernels  20.9 us (22%)
    ppermute x16, starting transfers between devices, shifted(): lax.ppermute(value, axis, [(i, (i + by) % count) for i in range(count)])  35.3 us
    ppermute x8, waiting for transfers between devices, partner(): return lax.ppermute(value, axis, [(i, i ^ bit) for i in range(count)])  19.2 us
    pallas_call x15, Pallas kernels, call(): pl.pallas_call(body, out_shape=tuple((jax.ShapeDtypeStruct(s, F32) for s...  18.3 us
    ppermute x8, starting transfers between devices, partner(): return lax.ppermute(value, axis, [(i, i ^ bit) for i in range(count)])  15.7 us
    ppermute x16, waiting for transfers between devices, shifted(): lax.ppermute(value, axis, [(i, (i + by) % count) for i in range(count)])  4.55 us
  transfers between devices with their start and end apart: 24, of which 8 were waited for; matrix products, arithmetic and copies ran while one was open for 0% of the time, Pallas kernels for 15%

commit v1 on v0

--- a/solution.py
+++ b/solution.py
@@ -44,7 +44,9 @@
     specs += [vmem()] * (len(ins) - smem - hbm)
     return pl.pallas_call(
       body,
-      out_shape=tuple(jax.ShapeDtypeStruct(s, F32) for s in outs),
+      out_shape=tuple(
+          o if isinstance(o, jax.ShapeDtypeStruct) else jax.ShapeDtypeStruct(o, F32) for o in outs
+      ),
       in_specs=specs,
       out_specs=tuple(vmem() for _ in outs),
       scratch_shapes=list(scratch),
@@ -75,10 +77,10 @@
     return high, low
 
 
-def physics_body(
-    count_ref, state_ref, level_ref, mix_ref, moved_ref,
-    raw_ref, sum_ref, s_ref, field_w, level_w,
-):
+PARTS = 2
+
+
+def field_weights(level_ref, mix_ref, field_w, level_w):
     high, low = field_operator(mix_ref[...])
     field_w[:, :96] = high
     field_w[:, 96:192] = low
@@ -86,46 +88,58 @@
     level_w[...] = jnp.zeros_like(level_w)
     level_w[:LEV, :LEV] = level_ref[...]
     level_w[LEV:, LEV:] = level_ref[...]
-    raw_ref[...] = state_ref[...]
-
+
+
+def turns(x_ref, field_w, level_w, rows):
     def part(row, half):
         return (slice(None), slice(16 * row + 8 * half, 16 * row + 8 * half + 8), slice(None))
 
-    def turn(rows):
-        now = [[raw_ref[part(r, h)].reshape(96, LEV) for h in range(2)] for r in rows]
-        packed = [jnp.concatenate([x.astype(BF16) for x in pair], axis=1) for pair in now]
-        mixed = jnp.dot(
-            jnp.concatenate(packed, axis=0), level_w[...], preferred_element_type=F32
+    now = [[x_ref[part(r, h)].reshape(96, LEV) for h in range(2)] for r in rows]
+    packed = [jnp.concatenate([x.astype(BF16) for x in pair], axis=1) for pair in now]
+    mixed = jnp.dot(jnp.concatenate(packed, axis=0), level_w[...], preferred_element_type=F32)
+    for i, r in enumerate(rows):
+        y = mixed[96 * i : 96 * i + 96]
+        y_high = y.astype(BF16)
+        y_low = (y[: 8 * EXTRA] - y_high[: 8 * EXTRA].astype(F32)).astype(BF16)
+        coupled = jnp.dot(
+            field_w[...],
+            jnp.concatenate([y_high, y_high, y_low], axis=0),
+            preferred_element_type=F32,
         )
-        for i, r in enumerate(rows):
-            y = mixed[96 * i : 96 * i + 96]
-            y_high = y.astype(BF16)
-            y_low = (y[: 8 * EXTRA] - y_high[: 8 * EXTRA].astype(F32)).astype(BF16)
-            coupled = jnp.dot(
-                field_w[...],
-                jnp.concatenate([y_high, y_high, y_low], axis=0),
-                preferred_element_type=F32,
-            )
-            for h in range(2):
-                value = jnp.tanh(coupled[:, LEV * h : LEV * h + LEV])
-                raw_ref[part(r, h)] = (0.5 * (now[i][h] + value)).reshape(NV, 8, LEV)
-
-    first = count_ref[0, 0]
-    second = count_ref[1, 0]
-    both = jnp.minimum(first, second)
+        for h in range(2):
+            value = jnp.tanh(coupled[:, LEV * h : LEV * h + LEV])
+            x_ref[part(r, h)] = (0.5 * (now[i][h] + value)).reshape(NV, 8, LEV)
+
+
+def joint_turns(index, count_ref, x_ref, field_w, level_w):
+    both = jnp.minimum(count_ref[0, 0], count_ref[1, 0])
 
     def joint(i, carry):
-        turn(range(16))
-        return carry
-
-    lax.fori_loop(0, both, joint, 0)
-    for block, count in ((0, first), (1, second)):
+        turns(x_ref, field_w, level_w, range(16))
+        return carry
+
+    lax.fori_loop(both * index // PARTS, both * (index + 1) // PARTS, joint, 0)
+    return both
+
+
+def physics_first(count_ref, state_ref, level_ref, mix_ref, x_ref, field_w, level_w):
+    field_weights(level_ref, mix_ref, field_w, level_w)
+    x_ref[...] = state_ref[...]
+    joint_turns(0, count_ref, x_ref, field_w, level_w)
+
+
+def physics_last(
+    count_ref, before_ref, field_w, level_w, state_ref, moved_ref, raw_ref, sum_ref, s_ref
+):
+    raw_ref[...] = before_ref[...]
+    both = joint_turns(PARTS - 1, count_ref, raw_ref, field_w, level_w)
+    for block in range(2):
 
         def single(i, carry, block=block):
-            turn(range(8 * block, 8 * block + 8))
+            turns(raw_ref, field_w, level_w, range(8 * block, 8 * block + 8))
             return carry
 
-        lax.fori_loop(both, count, single, 0)
+        lax.fori_loop(both, count_ref[block, 0], single, 0)
 
     def finish(v, carry):
         raw = raw_ref[v] - state_ref[v]
@@ -468,17 +482,24 @@
             pltpu.VMEM(slab, BF16), pltpu.VMEM(slab, BF16), pltpu.SemaphoreType.DMA((NV + 2,)),
         ),
     )
+    whole = (NV, 256, LEV)
     from_left, from_right = exchanged(left, right, "narrow")
-    (g,) = call(functools.partial(full_body, NV), (state, wxs, wys), ((NV, 256, LEV),), 3)
+    (g,) = call(functools.partial(full_body, NV), (state, wxs, wys), (whole,), 3)
     top, bottom, moved = call(
-        start_body, (state, g, from_left, from_right),
-        (edge12, edge12, (NV, 256, LEV)), 0.6,
+        start_body, (state, g, from_left, from_right), (edge12, edge12, whole), 0.6
     )
     above, below = exchanged(top, bottom, "wide")
+    x, field_w, level_w = call(
+        physics_first, (block_cost, state, level_mix, field_mix),
+        (
+            whole,
+            jax.ShapeDtypeStruct((96, 256), BF16),
+            jax.ShapeDtypeStruct((256, 256), BF16),
+        ), 8, smem=1,
+    )
     raw, total, s = call(
-        physics_body, (block_cost, state, level_mix, field_mix, moved),
-        ((NV, 256, LEV), (NV, LEV), (NF, 256, LEV)), 20,
-        scratch=(pltpu.VMEM((96, 256), BF16), pltpu.VMEM((256, 256), BF16)), smem=1,
+        physics_last, (block_cost, x, field_w, level_w, state, moved),
+        (whole, (NV, LEV), (NF, 256, LEV)), 8, smem=1,
     )
     more = partner(total, "wide", 8)
     plan = [

time: 96.8 us -> 98.1 us (1.013)
    pallas_call x15 -> x16, Pallas kernels: 18.3 us -> 19.1 us  [call(): pl.pallas_call(body, out_shape=tuple((o if isinstance(o, jax.ShapeDtypeSt...]
where the time goes in v1:
time: 98.1 us; the launch traced here: 97.9 us
  starting transfers between devices  51.4 us (52%)
  waiting for transfers between devices  23.8 us (24%)
  Pallas kernels  21.7 us (22%)
    ppermute x16, starting transfers between devices, shifted(): lax.ppermute(value, axis, [(i, (i + by) % count) for i in range(count)])  35.2 us
    ppermute x8, waiting for transfers between devices, partner(): return lax.ppermute(value, axis, [(i, i ^ bit) for i in range(count)])  19.2 us
    pallas_call x16, Pallas kernels, call(): pl.pallas_call(body, out_shape=tuple((o if isinstance(o, jax.ShapeDtypeSt...  19.1 us
    ppermute x8, starting transfers between devices, partner(): return lax.ppermute(value, axis, [(i, i ^ bit) for i in range(count)])  16.1 us
    ppermute x16, waiting for transfers between devices, shifted(): lax.ppermute(value, axis, [(i, (i + by) % count) for i in range(count)])  4.58 us
  transfers between devices with their start and end apart: 24, of which 8 were waited for; matrix products, arithmetic and copies ran while one was open for 0% of the time, Pallas kernels for 15%

profile of v1, /device:TPU:0, one launch (start us, length us, event | category | flops | bytes accessed | tf_op | source)
XLA Modules:
  0.0 97.9 jit_solution(1115621483747901741)
XLA Ops:
  0.6 2.0 %shard_map.77 = (f32[12,256,128]{2,1,0:T(8,128)S(1)}, f32[256,128]{1,0:T(8,128)S(1)}, f32[256,128]{1,0:T(8,128)S(1)}, f32[2,5,16,128]{3,2,1,0:T(8,128)S(1)}, f32...) custom-call(f32[12,256,128]{2,1,0:T(8,128)} %bitcast.6, bf16[256,128]{1,0:T(8,128)(2,1)} %bitcast.7, ...), custom_call_target="tpu_custom_call" | custom-call | flops 4000000 | bytes 2000000 | tf_op jit(solution)/shard_map/pallas_call | solution.py:45
  2.6 2.9 %collective-permute-start.1 = (f32[12,16,128]{2,1,0:T(8,128)S(1)}, f32[12,16,128]{2,1,0:T(8,128)S(1)}, u32[]{:S(2)}, u32[]{:S(2)}) collective-permute-start(f32[12,16,128]{2,1,0:T(8,128)S(1)} %get-tuple-element.53), channel_id=1, source_target_pairs={{0,7},{1,0},{2,1},{3,2},{4,3},{5,4},{6,5},{7,6},{8,15},{9,8},{10,9... | collective-permute-start | bytes 294920 | tf_op jit(solution)/shard_map/ppermute | solution.py:458
  8.9 1.6 %collective-permute-start.2 = (f32[12,16,128]{2,1,0:T(8,128)}, f32[12,16,128]{2,1,0:T(8,128)}, u32[]{:S(2)}, u32[]{:S(2)}) collective-permute-start(f32[12,16,128]{2,1,0:T(8,128)} %get-tuple-element.56), channel_id=1, source_target_pairs={{0,8},{8,16},{16,24},{24,32},{32,40},{40,48},{48,56},{56,64},{64,7... | collective-permute-start | bytes 294920 | tf_op jit(solution)/shard_map/ppermute | solution.py:458
  10.5 4.7 %collective-permute-start.3 = (f32[12,16,128]{2,1,0:T(8,128)}, f32[12,16,128]{2,1,0:T(8,128)}, u32[]{:S(2)}, u32[]{:S(2)}) collective-permute-start(f32[12,16,128]{2,1,0:T(8,128)} %get-tuple-element.57), channel_id=1, source_target_pairs={{0,120},{8,0},{16,8},{24,16},{32,24},{40,32},{48,40},{56,48},{64,5... | collective-permute-start | bytes 294920 | tf_op jit(solution)/shard_map/ppermute | solution.py:458
  15.4 3.6 %shard_map.78 = (f32[12,256,128]{2,1,0:T(8,128)S(1)}, bf16[96,256]{1,0:T(8,128)(2,1)S(1)}, bf16[256,256]{1,0:T(8,128)(2,1)S(1)}) custom-call(s32[2,1]{1,0:T(2,128)S(1)} %copy.10.count_ref, f32[12,256,128]{2,1,0:T(8,128)S(1)} %get-tuple-element.46.state_ref.s_ref, bf16[128,128]{1,0:T(8,128)(2,1)S(1)} %copy-done, f32[12,12]{1,0:T(8,128)S(1)} %copy-done.1), custom_call_target="tpu_custom_call" | custom-call | flops 32000000 | bytes 16000000 | tf_op jit(solution)/shard_map/pallas_call | solution.py:45
  19.0 3.7 %shard_map.81 = (f32[12,256,128]{2,1,0:T(8,128)S(1)}, f32[12,128]{1,0:T(8,128)S(1)}, f32[13,256,128]{2,1,0:T(8,128)S(1)}) custom-call(s32[2,1]{1,0:T(2,128)S(1)} %copy.10.count_ref, f32[12,256,128]{2,1,0:T(8,128)S(1)} %get-tuple-element.47.before_ref, bf16[96,256]{1,0:T(8,128)(2,1)S(1)} %get-tuple-element.48.field_w, ...), custom_call_target="tpu_custom_call" | custom-call | flops 32000000 | bytes 16000000 | tf_op jit(solution)/shard_map/pallas_call | solution.py:45
  22.6 1.5 %shard_map.82 = (f32[13,256,128]{2,1,0:T(8,128)S(1)}, f32[13,16,128]{2,1,0:T(8,128)S(1)}, f32[13,16,128]{2,1,0:T(8,128)S(1)}) custom-call(f32[13,256,128]{2,1,0:T(8,128)S(1)} %get-tuple-element.55.s_ref, f32[12,16,128]{2,1,0:T(8,128)} %collective-permute-done.2.above_ref, f32[12,16,128]{2,1,0:T(8,128)} %collective-permute-done.3.below_ref, ...), custom_call_target="tpu_custom_call" | custom-call | flops 2800000 | bytes 1400000 | tf_op jit(solution)/shard_map/pallas_call | solution.py:45
  24.9 3.1 %collective-permute-start.5 = (f32[13,16,128]{2,1,0:T(8,128)S(1)}, f32[13,16,128]{2,1,0:T(8,128)S(1)}, u32[]{:S(2)}, u32[]{:S(2)}) collective-permute-start(f32[13,16,128]{2,1,0:T(8,128)S(1)} %get-tuple-element.63), channel_id=1, source_target_pairs={{0,7},{1,0},{2,1},{3,2},{4,3},{5,4},{6,5},{7,6},{8,15},{9,8},{10,9... | collective-permute-start | bytes 319496 | tf_op jit(solution)/shard_map/ppermute | solution.py:458
  28.0 1.3 %shard_map.83 = (f32[13,256,128]{2,1,0:T(8,128)S(1)}, f32[12,128]{1,0:T(8,128)S(1)}) custom-call(f32[13,256,128]{2,1,0:T(8,128)S(1)} %get-tuple-element.59.s_ref, f32[256,128]{1,0:T(8,128)S(1)} %get-tuple-element.50.wxs_ref, f32[256,128]{1,0:T(8,128)S(1)} %get-tuple-element.51.wys_ref, f32[12,128]{1,0:T(8,128)S(1)} %get-tuple-element.60.refs_0_), custom_call_target="tpu_custom_call" | custom-call | flops 12000000 | bytes 6000000 | tf_op jit(solution)/shard_map/pallas_call | solution.py:45
  30.5 5.3 %collective-permute-start.8 = (f32[13,16,128]{2,1,0:T(8,128)S(1)}, f32[13,16,128]{2,1,0:T(8,128)S(1)}, u32[]{:S(2)}, u32[]{:S(2)}) collective-permute-start(f32[13,16,128]{2,1,0:T(8,128)S(1)} %get-tuple-element.68), channel_id=1, source_target_pairs={{0,120},{8,0},{16,8},{24,16},{32,24},{40,32},{48,40},{56,48},{64,5... | collective-permute-start | bytes 319496 | tf_op jit(solution)/shard_map/ppermute | solution.py:458
  35.8 14.3 %collective-permute-start.6 = (f32[12,128]{1,0:T(8,128)S(1)}, f32[12,128]{1,0:T(8,128)S(1)}, u32[]{:S(2)}, u32[]{:S(2)}) collective-permute-start(f32[12,128]{1,0:T(8,128)S(1)} %get-tuple-element.60.refs_0_), channel_id=1, source_target_pairs={{0,64},{8,72},{16,80},{24,88},{32,96},{40,104},{48,112},{56,120},{... | collective-permute-start | bytes 18440 | tf_op jit(solution)/shard_map/ppermute | solution.py:463
  50.1 1.6 %collective-permute-done.6 = f32[12,128]{1,0:T(8,128)S(1)} collective-permute-done((f32[12,128]{1,0:T(8,128)S(1)}, f32[12,128]{1,0:T(8,128)S(1)}, u32[]{:S(2)}, u32[]{:S(2)}) %collective-permute-start.6) | collective-permute-done | bytes 6176 | tf_op jit(solution)/shard_map/ppermute | solution.py:463
  52.8 2.9 %collective-permute-start.11 = (f32[13,16,128]{2,1,0:T(8,128)S(1)}, f32[13,16,128]{2,1,0:T(8,128)S(1)}, u32[]{:S(2)}, u32[]{:S(2)}) collective-permute-start(f32[13,16,128]{2,1,0:T(8,128)S(1)} %get-tuple-element.73), channel_id=1, source_target_pairs={{0,7},{1,0},{2,1},{3,2},{4,3},{5,4},{6,5},{7,6},{8,15},{9,8},{10,9... | collective-permute-start | bytes 319496 | tf_op jit(solution)/shard_map/ppermute | solution.py:458
  55.8 3.6 %collective-permute-done.9 = f32[12,128]{1,0:T(8,128)S(1)} collective-permute-done((f32[12,128]{1,0:T(8,128)S(1)}, f32[12,128]{1,0:T(8,128)S(1)}, u32[]{:S(2)}, u32[]{:S(2)}) %collective-permute-start.9) | collective-permute-done | bytes 6176 | tf_op jit(solution)/shard_map/ppermute | solution.py:463
  59.4 1.9 %collective-permute-start.12 = (f32[12,128]{1,0:T(8,128)S(1)}, f32[12,128]{1,0:T(8,128)S(1)}, u32[]{:S(2)}, u32[]{:S(2)}) collective-permute-start(f32[12,128]{1,0:T(8,128)S(1)} %add.22.refs_0_), channel_id=1, source_target_pairs={{0,1},{1,0},{2,3},{3,2},{4,5},{5,4},{6,7},{7,6},{8,9},{9,8},{10,11... | collective-permute-start | bytes 18440 | tf_op jit(solution)/shard_map/ppermute | solution.py:463
  62.8 5.3 %collective-permute-start.16 = (f32[13,16,128]{2,1,0:T(8,128)S(1)}, f32[13,16,128]{2,1,0:T(8,128)S(1)}, u32[]{:S(2)}, u32[]{:S(2)}) collective-permute-start(f32[13,16,128]{2,1,0:T(8,128)S(1)} %get-tuple-element.77), channel_id=1, source_target_pairs={{0,120},{8,0},{16,8},{24,16},{32,24},{40,32},{48,40},{56,48},{64,5... | collective-permute-start | bytes 319496 | tf_op jit(solution)/shard_map/ppermute | solution.py:458
  68.6 2.4 %collective-permute-done.15.above_ref = f32[13,16,128]{2,1,0:T(8,128)S(1)} collective-permute-done((f32[13,16,128]{2,1,0:T(8,128)S(1)}, f32[13,16,128]{2,1,0:T(8,128)S(1)}, u32[]{:S(2)}, u32[]{:S(2)}) %collective-permute-start.15) | collective-permute-done | bytes 106528 | tf_op jit(solution)/shard_map/ppermute | solution.py:458
  71.6 2.9 %collective-permute-start.19 = (f32[13,16,128]{2,1,0:T(8,128)S(1)}, f32[13,16,128]{2,1,0:T(8,128)S(1)}, u32[]{:S(2)}, u32[]{:S(2)}) collective-permute-start(f32[13,16,128]{2,1,0:T(8,128)S(1)} %get-tuple-element.82), channel_id=1, source_target_pairs={{0,7},{1,0},{2,1},{3,2},{4,3},{5,4},{6,5},{7,6},{8,15},{9,8},{10,9... | collective-permute-start | bytes 319496 | tf_op jit(solution)/shard_map/ppermute | solution.py:458
  74.5 5.2 %collective-permute-done.17 = f32[12,128]{1,0:T(8,128)S(1)} collective-permute-done((f32[12,128]{1,0:T(8,128)S(1)}, f32[12,128]{1,0:T(8,128)S(1)}, u32[]{:S(2)}, u32[]{:S(2)}) %collective-permute-start.17) | collective-permute-done | bytes 6176 | tf_op jit(solution)/shard_map/ppermute | solution.py:463
  79.7 1.3 %shard_map.91 = (f32[13,256,128]{2,1,0:T(8,128)S(1)}, f32[12,128]{1,0:T(8,128)S(1)}) custom-call(f32[13,256,128]{2,1,0:T(8,128)S(1)} %get-tuple-element.78.s_ref, f32[256,128]{1,0:T(8,128)S(1)} %get-tuple-element.50.wxs_ref, f32[256,128]{1,0:T(8,128)S(1)} %get-tuple-element.51.wys_ref, f32[12,128]{1,0:T(8,128)S(1)} %add.26.refs_0_), custom_call_target="tpu_custom_call" | custom-call | flops 12000000 | bytes 6000000 | tf_op jit(solution)/shard_map/pallas_call | solution.py:45
  81.2 5.3 %collective-permute-start.23 = (f32[13,16,128]{2,1,0:T(8,128)S(1)}, f32[13,16,128]{2,1,0:T(8,128)S(1)}, u32[]{:S(2)}, u32[]{:S(2)}) collective-permute-start(f32[13,16,128]{2,1,0:T(8,128)S(1)} %get-tuple-element.88), channel_id=1, source_target_pairs={{0,120},{8,0},{16,8},{24,16},{32,24},{40,32},{48,40},{56,48},{64,5... | collective-permute-start | bytes 319496 | tf_op jit(solution)/shard_map/ppermute | solution.py:458
  86.5 3.6 %collective-permute-done.20 = f32[12,128]{1,0:T(8,128)S(1)} collective-permute-done((f32[12,128]{1,0:T(8,128)S(1)}, f32[12,128]{1,0:T(8,128)S(1)}, u32[]{:S(2)}, u32[]{:S(2)}) %collective-permute-start.20) | collective-permute-done | bytes 6176 | tf_op jit(solution)/shard_map/ppermute | solution.py:463
  90.2 5.2 %collective-permute-done.21.more_ref = f32[12,128]{1,0:T(8,128)S(1)} collective-permute-done((f32[12,128]{1,0:T(8,128)S(1)}, f32[12,128]{1,0:T(8,128)S(1)}, u32[]{:S(2)}, u32[]{:S(2)}) %collective-permute-start.21) | collective-permute-done | bytes 6176 | tf_op jit(solution)/shard_map/ppermute | solution.py:463
  95.3 1.9 %output.1 = (f32[12,256,128]{2,1,0:T(8,128)}, f32[12,256,128]{2,1,0:T(8,128)}, f32[12,16,128]{2,1,0:T(8,128)S(1)}, f32[12,16,128]{2,1,0:T(8,128)S(1)}) custom-call(f32[13,256,128]{2,1,0:T(8,128)S(1)} %get-tuple-element.78.s_ref, f32[13,256,128]{2,1,0:T(8,128)S(1)} %get-tuple-element.80.g_ref, f32[13,16,128]{2,1,0:T(8,128)S(1)} %collective-permute-done.18.from_left, ...), custom_call_target="tpu_custom_call" | custom-call | flops 10000000 | bytes 8000000 | tf_op jit(solution)/shard_map/output/pallas_call | solution.py:407
  (54 shorter events, 9.9 us)
Async XLA Ops:
  2.6 5.3 %collective-permute-start = (f32[12,16,128]{2,1,0:T(8,128)S(1)}, f32[12,16,128]{2,1,0:T(8,128)S(1)}, u32[]{:S(2)}, u32[]{:S(2)}) collective-permute-start(f32[12,16,128]{2,1,0:T(8,128)S(1)} %get-tuple-element.52), channel_id=1, source_target_pairs={{0,1},{1,2},{2,3},{3,4},{4,5},{5,6},{6,7},{7,0},{8,9},{9,10},{10,1... | collective-permute-start | bytes 294920 | tf_op jit(solution)/shard_map/ppermute | solution.py:458
  2.6 5.2 %collective-permute-start.1 = (f32[12,16,128]{2,1,0:T(8,128)S(1)}, f32[12,16,128]{2,1,0:T(8,128)S(1)}, u32[]{:S(2)}, u32[]{:S(2)}) collective-permute-start(f32[12,16,128]{2,1,0:T(8,128)S(1)} %get-tuple-element.53), channel_id=1, source_target_pairs={{0,7},{1,0},{2,1},{3,2},{4,3},{5,4},{6,5},{7,6},{8,15},{9,8},{10,9... | collective-permute-start | bytes 294920 | tf_op jit(solution)/shard_map/ppermute | solution.py:458
  8.9 13.7 %collective-permute-start.2 = (f32[12,16,128]{2,1,0:T(8,128)}, f32[12,16,128]{2,1,0:T(8,128)}, u32[]{:S(2)}, u32[]{:S(2)}) collective-permute-start(f32[12,16,128]{2,1,0:T(8,128)} %get-tuple-element.56), channel_id=1, source_target_pairs={{0,8},{8,16},{16,24},{24,32},{32,40},{40,48},{48,56},{56,64},{64,7... | collective-permute-start | bytes 294920 | tf_op jit(solution)/shard_map/ppermute | solution.py:458
  10.5 12.1 %collective-permute-start.3 = (f32[12,16,128]{2,1,0:T(8,128)}, f32[12,16,128]{2,1,0:T(8,128)}, u32[]{:S(2)}, u32[]{:S(2)}) collective-permute-start(f32[12,16,128]{2,1,0:T(8,128)} %get-tuple-element.57), channel_id=1, source_target_pairs={{0,120},{8,0},{16,8},{24,16},{32,24},{40,32},{48,40},{56,48},{64,5... | collective-permute-start | bytes 294920 | tf_op jit(solution)/shard_map/ppermute | solution.py:458
  24.2 6.2 %collective-permute-start.4 = (f32[13,16,128]{2,1,0:T(8,128)S(1)}, f32[13,16,128]{2,1,0:T(8,128)S(1)}, u32[]{:S(2)}, u32[]{:S(2)}) collective-permute-start(f32[13,16,128]{2,1,0:T(8,128)S(1)} %get-tuple-element.62), channel_id=1, source_target_pairs={{0,1},{1,2},{2,3},{3,4},{4,5},{5,6},{6,7},{7,0},{8,9},{9,10},{10,1... | collective-permute-start | bytes 319496 | tf_op jit(solution)/shard_map/ppermute | solution.py:458
  24.9 5.4 %collective-permute-start.5 = (f32[13,16,128]{2,1,0:T(8,128)S(1)}, f32[13,16,128]{2,1,0:T(8,128)S(1)}, u32[]{:S(2)}, u32[]{:S(2)}) collective-permute-start(f32[13,16,128]{2,1,0:T(8,128)S(1)} %get-tuple-element.63), channel_id=1, source_target_pairs={{0,7},{1,0},{2,1},{3,2},{4,3},{5,4},{6,5},{7,6},{8,15},{9,8},{10,9... | collective-permute-start | bytes 319496 | tf_op jit(solution)/shard_map/ppermute | solution.py:458
  30.4 21.8 %collective-permute-start.7 = (f32[13,16,128]{2,1,0:T(8,128)S(1)}, f32[13,16,128]{2,1,0:T(8,128)S(1)}, u32[]{:S(2)}, u32[]{:S(2)}) collective-permute-start(f32[13,16,128]{2,1,0:T(8,128)S(1)} %get-tuple-element.67), channel_id=1, source_target_pairs={{0,8},{8,16},{16,24},{24,32},{32,40},{40,48},{48,56},{56,64},{64,7... | collective-permute-start | bytes 319496 | tf_op jit(solution)/shard_map/ppermute | solution.py:458
  30.5 21.7 %collective-permute-start.8 = (f32[13,16,128]{2,1,0:T(8,128)S(1)}, f32[13,16,128]{2,1,0:T(8,128)S(1)}, u32[]{:S(2)}, u32[]{:S(2)}) collective-permute-start(f32[13,16,128]{2,1,0:T(8,128)S(1)} %get-tuple-element.68), channel_id=1, source_target_pairs={{0,120},{8,0},{16,8},{24,16},{32,24},{40,32},{48,40},{56,48},{64,5... | collective-permute-start | bytes 319496 | tf_op jit(solution)/shard_map/ppermute | solution.py:458
  35.8 15.9 %collective-permute-start.6 = (f32[12,128]{1,0:T(8,128)S(1)}, f32[12,128]{1,0:T(8,128)S(1)}, u32[]{:S(2)}, u32[]{:S(2)}) collective-permute-start(f32[12,128]{1,0:T(8,128)S(1)} %get-tuple-element.60.refs_0_), channel_id=1, source_target_pairs={{0,64},{8,72},{16,80},{24,88},{32,96},{40,104},{48,112},{56,120},{... | collective-permute-start | bytes 18440 | tf_op jit(solution)/shard_map/ppermute | solution.py:463
  52.8 9.8 %collective-permute-start.10 = (f32[13,16,128]{2,1,0:T(8,128)S(1)}, f32[13,16,128]{2,1,0:T(8,128)S(1)}, u32[]{:S(2)}, u32[]{:S(2)}) collective-permute-start(f32[13,16,128]{2,1,0:T(8,128)S(1)} %get-tuple-element.72), channel_id=1, source_target_pairs={{0,1},{1,2},{2,3},{3,4},{4,5},{5,6},{6,7},{7,0},{8,9},{9,10},{10,1... | collective-permute-start | bytes 319496 | tf_op jit(solution)/shard_map/ppermute | solution.py:458
  52.8 9.8 %collective-permute-start.11 = (f32[13,16,128]{2,1,0:T(8,128)S(1)}, f32[13,16,128]{2,1,0:T(8,128)S(1)}, u32[]{:S(2)}, u32[]{:S(2)}) collective-permute-start(f32[13,16,128]{2,1,0:T(8,128)S(1)} %get-tuple-element.73), channel_id=1, source_target_pairs={{0,7},{1,0},{2,1},{3,2},{4,3},{5,4},{6,5},{7,6},{8,15},{9,8},{10,9... | collective-permute-start | bytes 319496 | tf_op jit(solution)/shard_map/ppermute | solution.py:458
  55.8 3.7 %collective-permute-start.9 = (f32[12,128]{1,0:T(8,128)S(1)}, f32[12,128]{1,0:T(8,128)S(1)}, u32[]{:S(2)}, u32[]{:S(2)}) collective-permute-start(f32[12,128]{1,0:T(8,128)S(1)} %add.21.sum_ref), channel_id=1, source_target_pairs={{0,32},{8,40},{16,48},{24,56},{32,0},{40,8},{48,16},{56,24},{64,96... | collective-permute-start | bytes 18440 | tf_op jit(solution)/shard_map/ppermute | solution.py:463
  59.4 8.7 %collective-permute-start.14 = (f32[12,128]{1,0:T(8,128)S(1)}, f32[12,128]{1,0:T(8,128)S(1)}, u32[]{:S(2)}, u32[]{:S(2)}) collective-permute-start(f32[12,128]{1,0:T(8,128)S(1)} %add.22.refs_0_), channel_id=1, source_target_pairs={{0,3},{1,2},{2,1},{3,0},{4,7},{5,6},{6,5},{7,4},{8,11},{9,10},{10,... | collective-permute-start | bytes 18440 | tf_op jit(solution)/shard_map/ppermute | solution.py:463
  59.4 8.7 %collective-permute-start.13 = (f32[12,128]{1,0:T(8,128)S(1)}, f32[12,128]{1,0:T(8,128)S(1)}, u32[]{:S(2)}, u32[]{:S(2)}) collective-permute-start(f32[12,128]{1,0:T(8,128)S(1)} %add.22.refs_0_), channel_id=1, source_target_pairs={{0,2},{1,3},{2,0},{3,1},{4,6},{5,7},{6,4},{7,5},{8,10},{9,11},{10,... | collective-permute-start | bytes 18440 | tf_op jit(solution)/shard_map/ppermute | solution.py:463
  59.4 8.7 %collective-permute-start.12 = (f32[12,128]{1,0:T(8,128)S(1)}, f32[12,128]{1,0:T(8,128)S(1)}, u32[]{:S(2)}, u32[]{:S(2)}) collective-permute-start(f32[12,128]{1,0:T(8,128)S(1)} %add.22.refs_0_), channel_id=1, source_target_pairs={{0,1},{1,0},{2,3},{3,2},{4,5},{5,4},{6,7},{7,6},{8,9},{9,8},{10,11... | collective-permute-start | bytes 18440 | tf_op jit(solution)/shard_map/ppermute | solution.py:463
  62.7 8.3 %collective-permute-start.15 = (f32[13,16,128]{2,1,0:T(8,128)S(1)}, f32[13,16,128]{2,1,0:T(8,128)S(1)}, u32[]{:S(2)}, u32[]{:S(2)}) collective-permute-start(f32[13,16,128]{2,1,0:T(8,128)S(1)} %get-tuple-element.76), channel_id=1, source_target_pairs={{0,8},{8,16},{16,24},{24,32},{32,40},{40,48},{48,56},{56,64},{64,7... | collective-permute-start | bytes 319496 | tf_op jit(solution)/shard_map/ppermute | solution.py:458
  62.8 8.2 %collective-permute-start.16 = (f32[13,16,128]{2,1,0:T(8,128)S(1)}, f32[13,16,128]{2,1,0:T(8,128)S(1)}, u32[]{:S(2)}, u32[]{:S(2)}) collective-permute-start(f32[13,16,128]{2,1,0:T(8,128)S(1)} %get-tuple-element.77), channel_id=1, source_target_pairs={{0,120},{8,0},{16,8},{24,16},{32,24},{40,32},{48,40},{56,48},{64,5... | collective-permute-start | bytes 319496 | tf_op jit(solution)/shard_map/ppermute | solution.py:458
  71.5 9.4 %collective-permute-start.18 = (f32[13,16,128]{2,1,0:T(8,128)S(1)}, f32[13,16,128]{2,1,0:T(8,128)S(1)}, u32[]{:S(2)}, u32[]{:S(2)}) collective-permute-start(f32[13,16,128]{2,1,0:T(8,128)S(1)} %get-tuple-element.81), channel_id=1, source_target_pairs={{0,1},{1,2},{2,3},{3,4},{4,5},{5,6},{6,7},{7,0},{8,9},{9,10},{10,1... | collective-permute-start | bytes 319496 | tf_op jit(solution)/shard_map/ppermute | solution.py:458
  71.6 9.4 %collective-permute-start.19 = (f32[13,16,128]{2,1,0:T(8,128)S(1)}, f32[13,16,128]{2,1,0:T(8,128)S(1)}, u32[]{:S(2)}, u32[]{:S(2)}) collective-permute-start(f32[13,16,128]{2,1,0:T(8,128)S(1)} %get-tuple-element.82), channel_id=1, source_target_pairs={{0,7},{1,0},{2,1},{3,2},{4,3},{5,4},{6,5},{7,6},{8,15},{9,8},{10,9... | collective-permute-start | bytes 319496 | tf_op jit(solution)/shard_map/ppermute | solution.py:458
  74.5 5.2 %collective-permute-start.17 = (f32[12,128]{1,0:T(8,128)S(1)}, f32[12,128]{1,0:T(8,128)S(1)}, u32[]{:S(2)}, u32[]{:S(2)}) collective-permute-start(f32[12,128]{1,0:T(8,128)S(1)} %add_add_fusion.sum_ref), channel_id=1, source_target_pairs={{0,16},{8,24},{16,0},{24,8},{32,48},{40,56},{48,32},{56,40},{64,80... | collective-permute-start | bytes 18440 | tf_op jit(solution)/shard_map/ppermute | solution.py:463
  81.1 16.1 %collective-permute-start.22 = (f32[13,16,128]{2,1,0:T(8,128)S(1)}, f32[13,16,128]{2,1,0:T(8,128)S(1)}, u32[]{:S(2)}, u32[]{:S(2)}) collective-permute-start(f32[13,16,128]{2,1,0:T(8,128)S(1)} %get-tuple-element.87), channel_id=1, source_target_pairs={{0,8},{8,16},{16,24},{24,32},{32,40},{40,48},{48,56},{56,64},{64,7... | collective-permute-start | bytes 319496 | tf_op jit(solution)/shard_map/ppermute | solution.py:458
  81.2 16.0 %collective-permute-start.23 = (f32[13,16,128]{2,1,0:T(8,128)S(1)}, f32[13,16,128]{2,1,0:T(8,128)S(1)}, u32[]{:S(2)}, u32[]{:S(2)}) collective-permute-start(f32[13,16,128]{2,1,0:T(8,128)S(1)} %get-tuple-element.88), channel_id=1, source_target_pairs={{0,120},{8,0},{16,8},{24,16},{32,24},{40,32},{48,40},{56,48},{64,5... | collective-permute-start | bytes 319496 | tf_op jit(solution)/shard_map/ppermute | solution.py:458
  86.5 3.7 %collective-permute-start.20 = (f32[12,128]{1,0:T(8,128)S(1)}, f32[12,128]{1,0:T(8,128)S(1)}, u32[]{:S(2)}, u32[]{:S(2)}) collective-permute-start(f32[12,128]{1,0:T(8,128)S(1)} %add.26.refs_0_), channel_id=1, source_target_pairs={{0,8},{8,0},{16,24},{24,16},{32,40},{40,32},{48,56},{56,48},{64,72... | collective-permute-start | bytes 18440 | tf_op jit(solution)/shard_map/ppermute | solution.py:463
  90.2 5.2 %collective-permute-start.21 = (f32[12,128]{1,0:T(8,128)S(1)}, f32[12,128]{1,0:T(8,128)S(1)}, u32[]{:S(2)}, u32[]{:S(2)}) collective-permute-start(f32[12,128]{1,0:T(8,128)S(1)} %add.27.sum_ref), channel_id=1, source_target_pairs={{0,4},{1,5},{2,6},{3,7},{4,0},{5,1},{6,2},{7,3},{8,12},{9,13},{10,... | collective-permute-start | bytes 18440 | tf_op jit(solution)/shard_map/ppermute | solution.py:463
  (3 other events, 25.7 us)
